TPU v7x, 128 devices: a whole 4x4x4 slice. The times are simulated.
128 devices in a mesh: dp: 64 (over y, x_lo, z, core), tensor: 2 (over x_hi).
Axes of the slice: x: 4 (x_hi: 2, x_lo: 2; x = x_hi * 2 + x_lo), y: 4, z: 4, core: 2. Of those that a mesh axis runs over, the one named last changes fastest.
Arguments:
- tokens: bfloat16 [64, 512, 896], P(None, 'dp'), may hold values from -6 to 6
- cotangent: bfloat16 [64, 512, 896], P(None, 'dp'), may hold values from -6 to 6
- lengths: int32 [64], replicated, may hold values from 1 to 512, 24576 in all
- deal_order: int32 [64], replicated, may hold values from 0 to 63, each once
- gain_attn: bfloat16 [896], replicated, may hold values from 0.099609375 to 1.8984375
- w_query: bfloat16 [896, 896], P(None, 'tensor'), may hold values from -0.1875 to 0.1875
- b_query: bfloat16 [896], P('tensor'), may hold values from -3 to 3
- w_key: bfloat16 [896, 128], P(None, 'tensor'), may hold values from -0.1875 to 0.1875
- b_key: bfloat16 [128], P('tensor'), may hold values from -3 to 3
- w_value: bfloat16 [896, 128], P(None, 'tensor'), may hold values from -0.1875 to 0.1875
- b_value: bfloat16 [128], P('tensor'), may hold values from -3 to 3
- w_out: bfloat16 [896, 896], P('tensor'), may hold values from -1 to 1
- gain_mlp: bfloat16 [896], replicated, may hold values from 0.099609375 to 1.8984375
- w_gate: bfloat16 [896, 4864], P(None, 'tensor'), may hold values from -0.1875 to 0.1875
- w_up: bfloat16 [896, 4864], P(None, 'tensor'), may hold values from -0.1875 to 0.1875
- w_down: bfloat16 [4864, 896], P('tensor'), may hold values from -0.078125 to 0.078125
Outputs:
- layer_out: bfloat16 [64, 512, 896], P(None, 'dp')
- grad_tokens: bfloat16 [64, 512, 896], P(None, 'dp')
- grad_gain_attn: float32 [896], replicated
- grad_w_query: float32 [896, 896], P(None, 'tensor')
- grad_b_query: float32 [896], P('tensor')
- grad_w_key: float32 [896, 128], P(None, 'tensor')
- grad_b_key: float32 [128], P('tensor')
- grad_w_value: float32 [896, 128], P(None, 'tensor')
- grad_b_value: float32 [128], P('tensor')
- grad_w_out: float32 [896, 896], P('tensor')
- grad_gain_mlp: float32 [896], replicated
- grad_w_gate: float32 [896, 4864], P(None, 'tensor')
- grad_w_up: float32 [896, 4864], P(None, 'tensor')
- grad_w_down: float32 [4864, 896], P('tensor')
- rms_values: float32 [3], replicated
Inputs may be any that keep to these rules, and one draw needn't show every extreme that they name: Group g receives stored slot deal_order[g]; every slot goes to exactly one group. The first lengths[g] rows of the slot that group g receives are valid.
All inputs are finite; a program needn't handle non-finite values.
Results may differ from a plain program's by a relative error of at most 0.022.
Values may be sent and summed in bfloat16 or wider, within the bound.
A program may use at most 192 MiB of HBM per device.

v0:
```python
import math
import jax
import jax.numpy as jnp
from jax import lax
from jax.sharding import PartitionSpec as P

HD = 64
epsilon = 1e-06
rope_base = 1000000.0


def rope_tables(seq_rows, head_size):
    places = jnp.arange(seq_rows).astype(jnp.float32)
    frequency = rope_base ** (-jnp.arange(head_size // 2).astype(jnp.float32) * 2.0 / head_size)
    angles = places[:, None] * frequency[None, :]
    return (jnp.cos(angles)[:, None, :], jnp.sin(angles)[:, None, :])


def rotate(tensor, cos_table, sine_table):
    half_width = tensor.shape[-1] // 2
    first_half = tensor[..., :half_width]
    second_half = tensor[..., half_width:]
    return jnp.concatenate(
        [
            first_half * cos_table - second_half * sine_table,
            second_half * cos_table + first_half * sine_table,
        ],
        axis=-1,
    )


def unrotate(grad_rot, cos_table, sine_table):
    half_width = grad_rot.shape[-1] // 2
    first_half = grad_rot[..., :half_width]
    second_half = grad_rot[..., half_width:]
    return jnp.concatenate(
        [
            first_half * cos_table + second_half * sine_table,
            second_half * cos_table - first_half * sine_table,
        ],
        axis=-1,
    )


def dot_left(matrix, other):
    return lax.dot_general(
        matrix, other, (((0,), (0,)), ((), ())), preferred_element_type=jnp.float32
    )


def dot_right(matrix, other):
    return lax.dot_general(
        matrix, other, (((1,), (1,)), ((), ())), preferred_element_type=jnp.float32
    )


def on_device(
    tokens,
    cotangent,
    lengths,
    deal_order,
    gain_attn,
    w_query,
    b_query,
    w_key,
    b_key,
    w_value,
    b_value,
    w_out,
    gain_mlp,
    w_gate,
    w_up,
    w_down,
):
    restore = jnp.argsort(deal_order)
    arrived = (
        lax.all_to_all(tokens[deal_order], "dp", split_axis=0, concat_axis=1, tiled=True),
        lax.all_to_all(cotangent[deal_order], "dp", split_axis=0, concat_axis=1, tiled=True),
    )
    stream = arrived[0][0].astype(jnp.float32)
    grad_out = arrived[1][0].astype(jnp.float32)
    seq_rows, width = stream.shape
    head_size = HD
    length = lengths[lax.axis_index("dp")]
    places = jnp.arange(seq_rows)
    usable = places < length
    row_mask = usable[:, None]
    cos_table, sine_table = rope_tables(seq_rows, head_size)
    local_heads = w_query.shape[1] // head_size
    local_kv = w_key.shape[1] // head_size
    group_size = local_heads // local_kv
    score_scale = 1.0 / math.sqrt(head_size)
    allowed = (places[None, :] <= places[:, None]) & usable[None, :]
    gain_one = gain_attn.astype(jnp.float32)
    gain_two = gain_mlp.astype(jnp.float32)
    inverse_one = lax.rsqrt(jnp.mean(stream * stream, axis=-1, keepdims=True) + epsilon)
    normed = (stream * inverse_one * gain_one).astype(jnp.bfloat16)
    q_lin = jnp.dot(normed, w_query, preferred_element_type=jnp.float32) + b_query.astype(
        jnp.float32
    )
    k_lin = jnp.dot(normed, w_key, preferred_element_type=jnp.float32) + b_key.astype(jnp.float32)
    v_lin = jnp.dot(normed, w_value, preferred_element_type=jnp.float32) + b_value.astype(
        jnp.float32
    )
    queries = rotate(q_lin.reshape(seq_rows, local_heads, head_size), cos_table, sine_table).astype(
        jnp.bfloat16
    )
    queries = queries.reshape(seq_rows, local_kv, group_size, head_size)
    keys_rot = rotate(k_lin.reshape(seq_rows, local_kv, head_size), cos_table, sine_table).astype(
        jnp.bfloat16
    )
    values = v_lin.reshape(seq_rows, local_kv, head_size).astype(jnp.bfloat16)
    raw_scores = jnp.einsum("qkgd,pkd->kgqp", queries, keys_rot, preferred_element_type=jnp.float32)
    scores = jnp.where(allowed, raw_scores * score_scale, -1e30)
    top_score = jnp.max(scores, axis=-1, keepdims=True)
    expo = jnp.exp(scores - top_score)
    total = jnp.sum(expo, axis=-1, keepdims=True)
    log_total = top_score + jnp.log(total)
    probs_low = (expo / total).astype(jnp.bfloat16)
    mixed = jnp.einsum("kgqp,pkd->qkgd", probs_low, values, preferred_element_type=jnp.float32)
    mixed = mixed.reshape(seq_rows, local_heads * head_size).astype(jnp.bfloat16)
    attention = lax.psum(jnp.dot(mixed, w_out, preferred_element_type=jnp.float32), "tensor")
    residual = stream + attention
    inverse_two = lax.rsqrt(jnp.mean(residual * residual, axis=-1, keepdims=True) + epsilon)
    normed_two = (residual * inverse_two * gain_two).astype(jnp.bfloat16)
    gate_lin = jnp.dot(normed_two, w_gate, preferred_element_type=jnp.float32)
    up_lin = jnp.dot(normed_two, w_up, preferred_element_type=jnp.float32)
    sigmoid_gate = jax.nn.sigmoid(gate_lin)
    silu_gate = gate_lin * sigmoid_gate
    hidden = (silu_gate * up_lin).astype(jnp.bfloat16)
    mlp_branch = lax.psum(
        jnp.dot(hidden, w_down, preferred_element_type=jnp.float32).astype(jnp.bfloat16), "tensor"
    ).astype(jnp.float32)
    result = jnp.where(row_mask, residual + mlp_branch, 0.0)
    statistics = jnp.stack(
        [
            jnp.sum(result * result),
            jnp.sum(jnp.where(row_mask, attention * attention, 0.0)),
            jnp.sum(jnp.where(row_mask, mlp_branch * mlp_branch, 0.0)),
        ]
    )
    grad_y = jnp.where(row_mask, grad_out, 0.0)
    grad_low = grad_y.astype(jnp.bfloat16)
    grad_w_down = dot_left(hidden, grad_low)
    grad_hidden = dot_right(grad_low, w_down)
    grad_gate = (
        grad_hidden * up_lin * sigmoid_gate * (1.0 + gate_lin * (1.0 - sigmoid_gate))
    ).astype(jnp.bfloat16)
    grad_up = (grad_hidden * silu_gate).astype(jnp.bfloat16)
    grad_w_gate = dot_left(normed_two, grad_gate)
    grad_w_up = dot_left(normed_two, grad_up)
    grad_normed_two = lax.psum(dot_right(grad_gate, w_gate) + dot_right(grad_up, w_up), "tensor")
    grad_gain_mlp = jnp.sum(grad_normed_two * residual * inverse_two, axis=0)
    scaled_two = grad_normed_two * gain_two
    grad_resid = (
        grad_y
        + inverse_two * scaled_two
        - residual * inverse_two**3 * jnp.mean(scaled_two * residual, axis=-1, keepdims=True)
    )
    grad_attn = grad_resid.astype(jnp.bfloat16)
    grad_w_out = dot_left(mixed, grad_attn)
    grad_mixed = dot_right(grad_attn, w_out).astype(jnp.bfloat16)
    grad_mixed = grad_mixed.reshape(seq_rows, local_kv, group_size, head_size)
    probs = jnp.exp(scores - log_total)
    grad_probs = jnp.einsum(
        "qkgd,pkd->kgqp", grad_mixed, values, preferred_element_type=jnp.float32
    )
    grad_values = jnp.einsum(
        "kgqp,qkgd->pkd", probs_low, grad_mixed, preferred_element_type=jnp.float32
    )
    row_inner = jnp.sum(probs * grad_probs, axis=-1, keepdims=True)
    grad_scores = (probs * (grad_probs - row_inner) * score_scale).astype(jnp.bfloat16)
    grad_queries = jnp.einsum(
        "kgqp,pkd->qkgd", grad_scores, keys_rot, preferred_element_type=jnp.float32
    )
    grad_keys = jnp.einsum(
        "kgqp,qkgd->pkd", grad_scores, queries, preferred_element_type=jnp.float32
    )
    grad_q_lin = unrotate(
        grad_queries.reshape(seq_rows, local_heads, head_size), cos_table, sine_table
    )
    grad_q_lin = grad_q_lin.reshape(seq_rows, local_heads * head_size).astype(jnp.bfloat16)
    grad_k_lin = (
        unrotate(grad_keys, cos_table, sine_table)
        .reshape(seq_rows, local_kv * head_size)
        .astype(jnp.bfloat16)
    )
    grad_v_lin = grad_values.reshape(seq_rows, local_kv * head_size).astype(jnp.bfloat16)
    grad_w_query = dot_left(normed, grad_q_lin)
    grad_w_key = dot_left(normed, grad_k_lin)
    grad_w_value = dot_left(normed, grad_v_lin)
    grad_b_query = jnp.sum(grad_q_lin.astype(jnp.float32), axis=0)
    grad_b_key = jnp.sum(grad_k_lin.astype(jnp.float32), axis=0)
    grad_b_value = jnp.sum(grad_v_lin.astype(jnp.float32), axis=0)
    grad_normed = lax.psum(
        (
            dot_right(grad_q_lin, w_query)
            + dot_right(grad_k_lin, w_key)
            + dot_right(grad_v_lin, w_value)
        ).astype(jnp.bfloat16),
        "tensor",
    ).astype(jnp.float32)
    grad_gain_attn = jnp.sum(grad_normed * stream * inverse_one, axis=0)
    scaled_one = grad_normed * gain_one
    grad_stream = (
        grad_resid
        + inverse_one * scaled_one
        - stream * inverse_one**3 * jnp.mean(scaled_one * stream, axis=-1, keepdims=True)
    )
    (
        statistics,
        grad_gain_attn,
        grad_w_query,
        grad_b_query,
        grad_w_key,
        grad_b_key,
        grad_w_value,
        grad_b_value,
        grad_w_out,
        grad_gain_mlp,
        grad_w_gate,
        grad_w_up,
        grad_w_down,
    ) = lax.psum(
        (
            statistics,
            grad_gain_attn,
            grad_w_query,
            grad_b_query,
            grad_w_key,
            grad_b_key,
            grad_w_value,
            grad_b_value,
            grad_w_out,
            grad_gain_mlp,
            grad_w_gate,
            grad_w_up,
            grad_w_down,
        ),
        "dp",
    )
    sent_back = (
        lax.all_to_all(
            result.astype(jnp.bfloat16)[None], "dp", split_axis=1, concat_axis=0, tiled=True
        ),
        lax.all_to_all(
            grad_stream.astype(jnp.bfloat16)[None], "dp", split_axis=1, concat_axis=0, tiled=True
        ),
    )
    layer_out = sent_back[0][restore]
    grad_tokens = sent_back[1][restore]
    count = jnp.sum(lengths).astype(jnp.float32) * width
    rms_values = jnp.sqrt(statistics / count)
    return (
        layer_out,
        grad_tokens,
        grad_gain_attn,
        grad_w_query,
        grad_b_query,
        grad_w_key,
        grad_b_key,
        grad_w_value,
        grad_b_value,
        grad_w_out,
        grad_gain_mlp,
        grad_w_gate,
        grad_w_up,
        grad_w_down,
        rms_values,
    )


def solution(mesh):
    in_specs = (
        P(None, "dp", None),
        P(None, "dp", None),
        P(),
        P(),
        P(),
        P(None, "tensor"),
        P("tensor"),
        P(None, "tensor"),
        P("tensor"),
        P(None, "tensor"),
        P("tensor"),
        P("tensor", None),
        P(),
        P(None, "tensor"),
        P(None, "tensor"),
        P("tensor", None),
    )
    out_specs = (
        P(None, "dp", None),
        P(None, "dp", None),
        P(),
        P(None, "tensor"),
        P("tensor"),
        P(None, "tensor"),
        P("tensor"),
        P(None, "tensor"),
        P("tensor"),
        P("tensor", None),
        P(),
        P(None, "tensor"),
        P(None, "tensor"),
        P("tensor", None),
        P(),
    )
    return jax.shard_map(
        on_device, mesh=mesh, in_specs=in_specs, out_specs=out_specs, check_vma=False
    )
```

profile of v0, /device:TPU:0, one launch (start us, length us, event | category | flops | bytes accessed | tf_op | source)
XLA Modules:
  0.0 1022.6 jit_solution(5831000406995036942)
XLA Ops:
  8.4 1.6 gather_fusion
  10.0 10.1 all-to-all-start
  22.0 14.5 %all-to-all-done = bf16[64,8,896]{2,1,0:T(8,128)(2,1)S(1)} async-done(((bf16[64,8,896]{2,1,0:T(8,128)(2,1)}), bf16[64,8,896]{2,1,0:T(8,128)(2,1)S(1)}, u32[]{:S(2)}, u32[]{:S(2)}) %all-to-all-start) | async-done | bytes 917536 | tf_op jit(solution)/shard_map/all_to_all | solution.py:77
  37.7 0.8 convolution_add_fusion.1
  38.7 1.3 fusion.6
  40.0 1.5 fusion.4
  42.1 0.8 copy-done.2
  42.9 2.3 fusion.36
  45.2 0.7 copy-done.8
  46.0 2.0 fusion.103
  48.0 1.6 gather_fusion.2
  49.6 5.5 all-to-all-start.2
  55.3 65.8 %all-reduce.8.cloned.1.call-done = f32[512,896]{1,0:T(8,128)} async-done(((f32[512,896]{1,0:T(8,128)}), f32[512,896]{1,0:T(8,128)}) %all-reduce.8.cloned.1.call-update) | async-done | bytes 1835024 | tf_op jit(solution)/shard_map/psum | solution.py:122
  121.1 1.8 multiply_reduce_fusion.3
  124.5 7.2 fusion.104
  131.7 4.5 fusion.105
  136.2 10.4 %multiply_convert_fusion = (bf16[512,2432]{1,0:T(8,128)(2,1)}, bf16[512,2432]{1,0:T(8,128)(2,1)}, bf16[512,2432]{1,0:T(8,128)(2,1)S(1)}) fusion(f32[512,2432]{1,0:T(8,128)} %fusion.104, f32[512,2432]{1,0:T(8,128)} %fusion.105, bf16[2432,896]{1,0:T(8,128)(2,1)} %param.31, bf16[64,8,896]{2,1,0:T(8,128)(2,1)} %all-to-all-done.2, ...), kind=kOutput, calls=%fused_computation.15 | convolution fusion | flops 2251423744 | bytes 22708736 | tf_op jit(solution)/shard_map/dot_general | solution.py:52
  146.6 1.5 copy-done.61
  148.0 6.0 convolution_convert_fusion
  154.1 6.0 fusion.106
  160.1 6.4 convolution_add_fusion
  167.7 8.2 fusion.108
  176.0 6.1 fusion.109
  182.1 7.5 fusion.65
  189.6 9.3 all-reduce.10.cloned.1.call-done
  198.9 67.2 %all-reduce.12.cloned.1.call-done = f32[512,896]{1,0:T(8,128)} async-done(((f32[512,896]{1,0:T(8,128)}), f32[512,896]{1,0:T(8,128)}) %all-reduce.12.cloned.1.call-update) | async-done | bytes 1835024 | tf_op jit(solution)/shard_map/psum | solution.py:152
  266.2 5.5 select_reduce_fusion
  271.8 2.5 fusion.35
  275.2 2.4 fusion
  277.6 2.4 fusion.7
  280.0 0.7 convolution_bitcast_fusion
  280.8 1.2 convolution_bitcast_fusion.1
  282.1 2.3 convert_reduce_fusion.1
  284.7 0.8 copy-done.15
  287.0 1.4 add_convert_fusion
  288.7 1.1 fusion.61
  289.8 1.1 fusion.63
  291.0 1.9 fusion.59
  292.9 1.8 fusion.56
  294.7 3.8 copy.64
  299.1 8.1 reduce.8
  307.2 2.9 reshape.436
  310.1 8.4 all-to-all-start.1
  318.5 22.4 %all-reduce.14.cloned.1.call-done = bf16[512,896]{1,0:T(8,128)(2,1)} async-done(((bf16[512,896]{1,0:T(8,128)(2,1)}), bf16[512,896]{1,0:T(8,128)(2,1)}) %all-reduce.14.cloned.1.call-update) | async-done | bytes 917520 | tf_op jit(solution)/shard_map/psum | solution.py:195
  340.9 2.0 fusion.29
  343.0 1.7 fusion.55
  344.7 1.4 copy.63
  346.1 6.2 reduce.9
  352.4 1.3 reshape.438
  353.7 8.3 all-to-all-start.3
  362.7 2.0 sort.17
  365.6 2.1 pad_maximum_fusion.3
  367.6 5.4 reshape.437
  373.0 1.0 copy.62
  374.1 2.8 gather_fusion.1
  376.8 280.9 %all-reduce = (f32[896]{0:T(1024)}, f32[448]{0:T(512)}, f32[64]{0:T(128)}, f32[64]{0:T(128)}, f32[896]{0:T(1024)}, /*index=5*/f32[3]{0:T(128)S(1)}) all-reduce(f32[896]{0:T(1024)S(1)} %get-tuple-element.20, f32[448]{0:T(512)S(1)} %reduce_sum.145, f32[64]{0:T(128)S(1)} %convert_reduce_fusion.2, ...), channel_id=1, replica_groups=mesh['dp'=64,'tensor'=2] {'dp'}, use_global_device_ids=true, to_apply=%region_13.14 | all-reduce | flops 2371 | bytes 18968 | tf_op jit(solution)/shard_map/psum | solution.py:224
  659.1 1.6 gather_fusion.3
  660.7 331.3 %all-reduce.16.cloned.1.call-done = (f32[896,448]{0,1:T(8,128)}, f32[896,64]{0,1:T(8,128)}, f32[896,64]{0,1:T(8,128)}, f32[448,896]{1,0:T(8,128)}, f32[896,2432]...) async-done(((f32[896,448]{0,1:T(8,128)}, f32[896,64]{0,1:T(8,128)}, f32[896,64]{0,1:T(8,128)}, f32[448,896]{1,0:T(8,128)}, f32[896,2432]{1,0:T(8,128)}, ...) | async-done | bytes 29818896 | tf_op jit(solution)/shard_map/psum | solution.py:224
  992.0 2.8 copy.76
  996.2 1.2 copy.79
  997.4 8.6 copy.80
  1006.0 4.4 copy.81
  1010.4 1.6 slice-done.3
  1012.1 3.5 copy.82
  (199 shorter events, 15.1 us)
Async XLA Ops:
  7.2 12.9 %copy-start.56 = (bf16[64]{0:T(256)(128)(2,1)S(1)}, bf16[64]{0:T(256)(128)(2,1)}, u32[]{:S(2)}) copy-start(bf16[64]{0:T(256)(128)(2,1)} %param.26) | copy-start | bytes 388
  7.2 12.9 %copy-start.53 = (bf16[896]{0:T(1024)(128)(2,1)S(1)}, bf16[896]{0:T(1024)(128)(2,1)}, u32[]{:S(2)}) copy-start(bf16[896]{0:T(1024)(128)(2,1)} %param.20) | copy-start | bytes 5380
  7.2 13.0 %copy-start.55 = (bf16[448]{0:T(512)(128)(2,1)S(1)}, bf16[448]{0:T(512)(128)(2,1)}, u32[]{:S(2)}) copy-start(bf16[448]{0:T(512)(128)(2,1)} %param.22) | copy-start | bytes 2692
  7.2 13.0 %copy-start.57 = (bf16[64]{0:T(256)(128)(2,1)S(1)}, bf16[64]{0:T(256)(128)(2,1)}, u32[]{:S(2)}) copy-start(bf16[64]{0:T(256)(128)(2,1)} %param.24) | copy-start | bytes 388
  7.2 13.0 %copy-start.58 = (s32[64]{0:T(128)S(1)}, s32[64]{0:T(128)}, u32[]{:S(2)}) copy-start(s32[64]{0:T(128)} %param.18) | copy-start | bytes 772
  8.4 28.5 %copy-start.26 = (bf16[896,64]{0,1:T(8,128)(2,1)S(1)}, bf16[896,64]{0,1:T(8,128)(2,1)}, u32[]{:S(2)}) copy-start(bf16[896,64]{0,1:T(8,128)(2,1)} %param.23) | copy-start | bytes 344068
  10.0 27.7 %copy-start.14 = (bf16[896,448]{0,1:T(8,128)(2,1)S(1)}, bf16[896,448]{0,1:T(8,128)(2,1)}, u32[]{:S(2)}) copy-start(bf16[896,448]{0,1:T(8,128)(2,1)} %param.21) | copy-start | bytes 2408452
  10.0 26.5 %all-to-all-start = ((bf16[64,8,896]{2,1,0:T(8,128)(2,1)}), bf16[64,8,896]{2,1,0:T(8,128)(2,1)S(1)}, u32[]{:S(2)}, u32[]{:S(2)}) async-start(bf16[64,8,896]{2,1,0:T(8,128)(2,1)} %gather_fusion), calls=%async_computation | async-start | bytes 1835008 | tf_op jit(solution)/shard_map/all_to_all | solution.py:77
  20.1 101.1 %all-reduce.8.cloned.1.call-start = ((), (), s32[]{:S(2)}) async-start(), calls=%async_computation.4 | async-start | bytes 3670016 | tf_op jit(solution)/shard_map/psum | solution.py:122
  20.2 21.4 %copy-start.38 = (f32[896]{0:T(1024)}, f32[896]{0:T(1024)S(1)}, u32[]{:S(2)}) copy-start(f32[896]{0:T(1024)S(1)} %convert_element_type.242) | copy-start | bytes 10756
  20.8 17.7 %copy-start.48 = (f32[32]{0:T(128)}, f32[32]{0:T(128)S(1)}, u32[]{:S(2)}) copy-start(f32[32]{0:T(128)S(1)} %multiply_power_fusion) | copy-start | bytes 388
  21.5 114.7 %copy-start.50 = (pred[512]{0:T(512)(128)(4,1)}, pred[512]{0:T(512)(128)(4,1)S(1)}, u32[]{:S(2)}) copy-start(pred[512]{0:T(512)(128)(4,1)S(1)} %iota_compare_fusion.1) | copy-start | bytes 1540
  21.5 17.0 %copy-start.42 = (f32[512]{0:T(512)}, f32[512]{0:T(512)S(1)}, u32[]{:S(2)}) copy-start(f32[512]{0:T(512)S(1)} %iota_convert_fusion) | copy-start | bytes 6148
  21.8 16.7 %copy-start.16 = (f32[512,32]{0,1:T(8,128)}, f32[512,32]{0,1:T(8,128)S(1)}, u32[]{:S(2)}) copy-start(f32[512,32]{0,1:T(8,128)S(1)} %get-tuple-element.58) | copy-start | bytes 196612
  36.9 4.7 copy-start.44
  37.7 2.3 copy-start.22
  37.7 2.3 copy-start.24
  40.0 2.9 copy-start.2
  40.0 2.9 copy-start.34
  41.6 3.6 copy-start.36
  42.9 3.1 copy-start.6
  45.2 2.7 copy-start.11
  47.9 7.4 copy-start.54
  49.6 86.6 %all-to-all-start.2 = ((bf16[64,8,896]{2,1,0:T(8,128)(2,1)}), bf16[64,8,896]{2,1,0:T(8,128)(2,1)}, u32[]{:S(2)}, u32[]{:S(2)}) async-start(bf16[64,8,896]{2,1,0:T(8,128)(2,1)} %gather_fusion.2), calls=%async_computation.2 | async-start | bytes 1835008 | tf_op jit(solution)/shard_map/all_to_all | solution.py:78
  55.0 143.9 %all-reduce.10.cloned.1.call-start = ((), (), s32[]{:S(2)}) async-start(), calls=%async_computation.5 | async-start | bytes 1835008 | tf_op jit(solution)/shard_map/psum | solution.py:131
  55.3 69.1 %copy-start.32 = (f32[896]{0:T(1024)}, f32[896]{0:T(1024)S(1)}, u32[]{:S(2)}) copy-start(f32[896]{0:T(1024)S(1)} %convert_element_type.255) | copy-start | bytes 10756
  123.0 143.2 %copy-start.3 = (f32[512,896]{1,0:T(8,128)}, f32[512,896]{1,0:T(8,128)S(1)}, u32[]{:S(2)}) copy-start(f32[512,896]{1,0:T(8,128)S(1)} %get-tuple-element.40) | copy-start | bytes 5505028
  124.2 7.5 slice-start.5
  124.4 7.2 copy-start.12
  124.5 7.2 slice-start.6
  154.1 112.1 %all-reduce.12.cloned.1.call-start = ((), (), s32[]{:S(2)}) async-start(), calls=%async_computation.6 | async-start | bytes 3670016 | tf_op jit(solution)/shard_map/psum | solution.py:152
  154.1 6.0 copy-start.63
  166.5 174.5 %all-reduce.14.cloned.1.call-start = ((), (), s32[]{:S(2)}) async-start(), calls=%async_computation.7 | async-start | bytes 1835008 | tf_op jit(solution)/shard_map/psum | solution.py:195
  167.7 8.3 copy-start.13
  167.7 8.3 copy-start.64
  175.9 6.1 copy-start.51
  175.9 6.1 copy-start.62
  266.1 5.6 copy-start.5
  266.1 5.6 copy-start.33
  266.1 5.6 copy-start.41
  266.1 5.6 copy-start.47
  266.1 5.6 copy-start.52
  266.2 8.8 slice-start
  271.7 2.5 copy-start.7
  271.8 3.2 slice-start.1
  277.6 2.4 copy-start.23
  277.6 2.4 copy-start.25
  282.0 2.3 copy-start.17
  288.4 703.6 %all-reduce.16.cloned.1.call-start = ((), (), s32[]{:S(2)}) async-start(), calls=%async_computation.8 | async-start | bytes 59637760 | tf_op jit(solution)/shard_map/psum | solution.py:224
  289.8 3.0 copy-start.9
  307.2 11.3 %copy-start.45 = (f32[512]{0:T(512)S(1)}, f32[512]{0:T(512)}, u32[]{:S(2)}) copy-start(f32[512]{0:T(512)} %copy-done.44) | copy-start | bytes 6148
  310.1 43.6 %all-to-all-start.1 = ((bf16[64,2,3584]{2,1,0:T(2,128)(2,1)}), bf16[64,2,3584]{2,1,0:T(2,128)(2,1)}, u32[]{:S(2)}, u32[]{:S(2)}) async-start(bf16[64,2,3584]{2,1,0:T(2,128)(2,1)} %reshape.436), calls=%async_computation.1 | async-start | bytes 1835008 | tf_op jit(solution)/shard_map/all_to_all | solution.py:243
  352.4 9.6 copy-start.59
  352.4 10.3 %copy-start.60 = (s32[64]{0:T(128)S(1)}, s32[64]{0:T(128)}, u32[]{:S(2)}) copy-start(s32[64]{0:T(128)} %param.19) | copy-start | bytes 772
  353.7 304.6 %all-to-all-start.3 = ((bf16[64,2,3584]{2,1,0:T(2,128)(2,1)}), bf16[64,2,3584]{2,1,0:T(2,128)(2,1)S(1)}, u32[]{:S(2)}, u32[]{:S(2)}) async-start(bf16[64,2,3584]{2,1,0:T(2,128)(2,1)} %reshape.438), calls=%async_computation.3 | async-start | bytes 1835008 | tf_op jit(solution)/shard_map/all_to_all | solution.py:246
  373.0 3.8 copy-start.46
  992.0 2.8 copy-start.21
  992.0 3.5 copy-start.20
  992.0 4.2 copy-start.10
  997.4 8.6 copy-start.4
  997.4 13.0 %slice-start.2 = ((s8[8716288]{0:T(1024)(128)(4,1)}), s8[4194304]{0:T(1024)(128)(4,1)S(1)}, s32[]{:S(2)}) async-start(s8[8716288]{0:T(1024)(128)(4,1)} %bitcast.213), calls=%async_computation.11 | async-start | bytes 8388608
  997.4 14.6 %slice-start.3 = ((s8[8716288]{0:T(1024)(128)(4,1)}), s8[4194304]{0:T(1024)(128)(4,1)S(1)}, s32[]{:S(2)}) async-start(s8[8716288]{0:T(1024)(128)(4,1)} %bitcast.213), calls=%async_computation.12 | async-start | bytes 8388608
  1006.0 6.1 slice-start.4
  1012.1 3.5 copy-start.1
  (17 other events, 24.8 us)
Sparse Core Ops, SparseCore 0:
  48.1 73.0 all-reduce.7
  154.2 44.6 all-reduce.9
  201.4 64.7 all-reduce.11
  288.6 52.3 all-reduce.13
  345.0 646.9 all-reduce.15
where the time goes:
time: 1030 us; the launch traced here: 1020 us
  waiting for transfers between devices  511 us (50%)
  blocking collectives  281 us (27%)
  matrix products  85.3 us (8%)
  local copies, waits for them, and re-layouts  54.4 us (5%)
  other arithmetic  42 us (4%)
  starting transfers between devices  33.3 us (3%)
  between operations  16 us (2%)
    psum x1, waiting for transfers between devices, on_device(): lax.psum((statistics, grad_gain_attn, grad_w_query, grad_b_query, grad_w_...  331 us
    psum x1, blocking collectives, on_device(): lax.psum((statistics, grad_gain_attn, grad_w_query, grad_b_query, grad_w_...  281 us
    psum x1, waiting for transfers between devices, on_device(): lax.psum(dot_right(grad_gate, w_gate) + dot_right(grad_up, w_up), 'tensor')  67.2 us
    psum x1, waiting for transfers between devices, on_device(): lax.psum(jnp.dot(mixed, w_out, preferred_element_type=jnp.float32), 'tens...  65.8 us
    unnamed x158, local copies, waits for them, and re-layouts  40.9 us
    dot_general x7, matrix products, dot_left(): lax.dot_general(matrix, other, (((0,), (0,)), ((), ())), preferred_elemen...  27.9 us
    dot_general x7, matrix products, dot_right(): lax.dot_general(matrix, other, (((1,), (1,)), ((), ())), preferred_elemen...  25.9 us
    psum x1, waiting for transfers between devices, on_device(): lax.psum((dot_right(grad_q_lin, w_query) + dot_right(grad_k_lin, w_key) +...  22.4 us
  transfers between devices with their start and end apart: 9, of which 6 were waited for; matrix products, arithmetic and copies ran while one was open for 10% of the time, Pallas kernels for 0%

commit v1 on v0

--- a/solution.py
+++ b/solution.py
@@ -7,6 +7,12 @@
 HD = 64
 epsilon = 1e-06
 rope_base = 1000000.0
+
+
+def exchange_blocks(x, axis, split, join):
+    pieces = jnp.split(x, lax.axis_size(axis), axis=split)
+    received = lax.all_to_all(jnp.stack(pieces), axis, 0, 0)
+    return jnp.concatenate(received, axis=join)
 
 
 def rope_tables(seq_rows, head_size):
@@ -74,7 +80,7 @@
 ):
     restore = jnp.argsort(deal_order)
     arrived = (
-        lax.all_to_all(tokens[deal_order], "dp", split_axis=0, concat_axis=1, tiled=True),
+        exchange_blocks(tokens[deal_order], "dp", 0, 1),
         lax.all_to_all(cotangent[deal_order], "dp", split_axis=0, concat_axis=1, tiled=True),
     )
     stream = arrived[0][0].astype(jnp.float32)

time: 1030 us -> 1070 us (1.039)
  local copies, waits for them, and re-layouts: 54.4 us -> 92 us
    unnamed x158 -> x221, local copies, waits for them, and re-layouts: 40.9 us -> 78.8 us
where the time goes in v1:
time: 1070 us; the launch traced here: 1060 us
  waiting for transfers between devices  511 us (48%)
  blocking collectives  281 us (26%)
  local copies, waits for them, and re-layouts  92 us (9%)
  matrix products  85.3 us (8%)
  other arithmetic  42 us (4%)
  starting transfers between devices  33.3 us (3%)
  between operations  16 us (1%)
    psum x1, waiting for transfers between devices, on_device(): lax.psum((statistics, grad_gain_attn, grad_w_query, grad_b_query, grad_w_...  331 us
    psum x1, blocking collectives, on_device(): lax.psum((statistics, grad_gain_attn, grad_w_query, grad_b_query, grad_w_...  281 us
    unnamed x221, local copies, waits for them, and re-layouts  78.8 us
    psum x1, waiting for transfers between devices, on_device(): lax.psum(dot_right(grad_gate, w_gate) + dot_right(grad_up, w_up), 'tensor')  67.2 us
    psum x1, waiting for transfers between devices, on_device(): lax.psum(jnp.dot(mixed, w_out, preferred_element_type=jnp.float32), 'tens...  65.8 us
    dot_general x7, matrix products, dot_left(): lax.dot_general(matrix, other, (((0,), (0,)), ((), ())), preferred_elemen...  27.8 us
    dot_general x7, matrix products, dot_right(): lax.dot_general(matrix, other, (((1,), (1,)), ((), ())), preferred_elemen...  25.9 us
    psum x1, waiting for transfers between devices, on_device(): lax.psum((dot_right(grad_q_lin, w_query) + dot_right(grad_k_lin, w_key) +...  22.4 us
  transfers between devices with their start and end apart: 9, of which 6 were waited for; matrix products, arithmetic and copies ran while one was open for 10% of the time, Pallas kernels for 0%

profile of v1, /device:TPU:0, one launch (start us, length us, event | category | flops | bytes accessed | tf_op | source)
XLA Modules:
  0.0 1060.2 jit_solution(10512626835295975462)
XLA Ops:
  47.6 10.1 all-to-all-start
  59.6 14.5 %all-to-all-done = bf16[64,1,8,896]{3,2,1,0:T(8,128)(2,1)S(1)} async-done(((bf16[64,1,8,896]{3,2,1,0:T(8,128)(2,1)}), bf16[64,1,8,896]{3,2,1,0:T(8,128)(2,1)S(1)}, u32[]{:S(2)}, u32[]{:S(2)}) %all-to-all-start) | async-done | bytes 917536 | tf_op jit(solution)/shard_map/all_to_all | solution.py:14
  75.4 0.8 convolution_add_fusion.1
  76.3 1.3 fusion.6
  77.7 1.5 fusion.4
  79.8 0.8 copy-done.2
  80.6 2.3 fusion.36
  82.9 0.7 copy-done.8
  83.6 2.0 fusion.103
  85.6 1.6 gather_fusion.2
  87.2 5.5 all-to-all-start.2
  93.0 65.8 %all-reduce.8.cloned.1.call-done = f32[512,896]{1,0:T(8,128)} async-done(((f32[512,896]{1,0:T(8,128)}), f32[512,896]{1,0:T(8,128)}) %all-reduce.8.cloned.1.call-update) | async-done | bytes 1835024 | tf_op jit(solution)/shard_map/psum | solution.py:128
  158.8 1.8 multiply_reduce_fusion.3
  162.1 7.2 fusion.104
  169.3 4.5 fusion.105
  173.8 10.4 multiply_convert_fusion
  184.2 1.5 copy-done.61
  185.7 6.0 convolution_convert_fusion
  191.8 6.0 fusion.106
  197.8 6.4 convolution_add_fusion
  204.6 0.7 log_add_fusion
  205.4 8.2 fusion.108
  213.6 6.1 fusion.109
  219.7 7.5 fusion.65
  227.3 9.3 all-reduce.10.cloned.1.call-done
  236.6 67.2 %all-reduce.12.cloned.1.call-done = f32[512,896]{1,0:T(8,128)} async-done(((f32[512,896]{1,0:T(8,128)}), f32[512,896]{1,0:T(8,128)}) %all-reduce.12.cloned.1.call-update) | async-done | bytes 1835024 | tf_op jit(solution)/shard_map/psum | solution.py:158
  303.8 5.5 select_reduce_fusion
  309.4 2.5 fusion.35
  312.8 2.4 fusion
  315.3 2.4 fusion.7
  317.7 0.7 convolution_bitcast_fusion
  318.5 1.2 convolution_bitcast_fusion.1
  319.7 2.3 convert_reduce_fusion.1
  322.4 0.8 copy-done.15
  324.7 1.4 add_convert_fusion
  326.4 1.1 fusion.61
  327.5 1.1 fusion.63
  328.6 1.9 fusion.59
  330.5 1.8 fusion.56
  332.4 3.8 copy.64
  336.7 8.1 reduce.6
  344.8 2.9 reshape.425
  347.7 8.4 all-to-all-start.1
  356.2 22.4 %all-reduce.14.cloned.1.call-done = bf16[512,896]{1,0:T(8,128)(2,1)} async-done(((bf16[512,896]{1,0:T(8,128)(2,1)}), bf16[512,896]{1,0:T(8,128)(2,1)}) %all-reduce.14.cloned.1.call-update) | async-done | bytes 917520 | tf_op jit(solution)/shard_map/psum | solution.py:201
  378.6 2.0 fusion.29
  380.6 1.7 fusion.55
  382.3 1.4 copy.63
  383.8 6.2 reduce.7
  390.0 1.3 reshape.427
  391.3 8.3 all-to-all-start.3
  400.3 2.0 sort.17
  403.2 2.1 pad_maximum_fusion.3
  405.3 5.4 reshape.426
  410.7 1.0 copy.62
  411.7 2.8 gather_fusion.1
  414.5 280.9 %all-reduce = (f32[896]{0:T(1024)}, f32[448]{0:T(512)}, f32[64]{0:T(128)}, f32[64]{0:T(128)}, f32[896]{0:T(1024)}, /*index=5*/f32[3]{0:T(128)S(1)}) all-reduce(f32[896]{0:T(1024)S(1)} %get-tuple-element.20, f32[448]{0:T(512)S(1)} %reduce_sum.145, f32[64]{0:T(128)S(1)} %convert_reduce_fusion.2, ...), channel_id=1, replica_groups=mesh['dp'=64,'tensor'=2] {'dp'}, use_global_device_ids=true, to_apply=%region_13.14 | all-reduce | flops 2371 | bytes 18968 | tf_op jit(solution)/shard_map/psum | solution.py:230
  696.8 1.6 gather_fusion.3
  698.4 331.3 %all-reduce.16.cloned.1.call-done = (f32[896,448]{0,1:T(8,128)}, f32[896,64]{0,1:T(8,128)}, f32[896,64]{0,1:T(8,128)}, f32[448,896]{1,0:T(8,128)}, f32[896,2432]...) async-done(((f32[896,448]{0,1:T(8,128)}, f32[896,64]{0,1:T(8,128)}, f32[896,64]{0,1:T(8,128)}, f32[448,896]{1,0:T(8,128)}, f32[896,2432]{1,0:T(8,128)}, ...) | async-done | bytes 29818896 | tf_op jit(solution)/shard_map/psum | solution.py:230
  1029.7 2.8 copy.139
  1033.9 1.2 copy.142
  1035.0 8.6 copy.143
  1043.7 4.4 copy.144
  1048.1 1.6 slice-done.3
  1049.8 3.5 copy.145
  (263 shorter events, 53.6 us)
Async XLA Ops:
  8.4 49.4 %copy-start.56 = (bf16[64]{0:T(256)(128)(2,1)S(1)}, bf16[64]{0:T(256)(128)(2,1)}, u32[]{:S(2)}) copy-start(bf16[64]{0:T(256)(128)(2,1)} %param.26) | copy-start | bytes 388
  8.4 49.4 %copy-start.53 = (bf16[896]{0:T(1024)(128)(2,1)S(1)}, bf16[896]{0:T(1024)(128)(2,1)}, u32[]{:S(2)}) copy-start(bf16[896]{0:T(1024)(128)(2,1)} %param.20) | copy-start | bytes 5380
  8.4 49.4 %copy-start.55 = (bf16[448]{0:T(512)(128)(2,1)S(1)}, bf16[448]{0:T(512)(128)(2,1)}, u32[]{:S(2)}) copy-start(bf16[448]{0:T(512)(128)(2,1)} %param.22) | copy-start | bytes 2692
  8.4 49.5 %copy-start.57 = (bf16[64]{0:T(256)(128)(2,1)S(1)}, bf16[64]{0:T(256)(128)(2,1)}, u32[]{:S(2)}) copy-start(bf16[64]{0:T(256)(128)(2,1)} %param.24) | copy-start | bytes 388
  8.4 49.5 %copy-start.58 = (s32[64]{0:T(128)S(1)}, s32[64]{0:T(128)}, u32[]{:S(2)}) copy-start(s32[64]{0:T(128)} %param.18) | copy-start | bytes 772
  12.7 61.8 %copy-start.26 = (bf16[896,64]{0,1:T(8,128)(2,1)S(1)}, bf16[896,64]{0,1:T(8,128)(2,1)}, u32[]{:S(2)}) copy-start(bf16[896,64]{0,1:T(8,128)(2,1)} %param.23) | copy-start | bytes 344068
  47.6 27.7 %copy-start.14 = (bf16[896,448]{0,1:T(8,128)(2,1)S(1)}, bf16[896,448]{0,1:T(8,128)(2,1)}, u32[]{:S(2)}) copy-start(bf16[896,448]{0,1:T(8,128)(2,1)} %param.21) | copy-start | bytes 2408452
  47.6 26.5 %all-to-all-start = ((bf16[64,1,8,896]{3,2,1,0:T(8,128)(2,1)}), bf16[64,1,8,896]{3,2,1,0:T(8,128)(2,1)S(1)}, u32[]{:S(2)}, u32[]{:S(2)}) async-start(bf16[64,1,8,896]{3,2,1,0:T(8,128)(2,1)} %constant_dynamic-update-slice_fusion), calls=%async_computation | async-start | bytes 1835008 | tf_op jit(solution)/shard_map/all_to_all | solution.py:14
  57.7 101.1 %all-reduce.8.cloned.1.call-start = ((), (), s32[]{:S(2)}) async-start(), calls=%async_computation.4 | async-start | bytes 3670016 | tf_op jit(solution)/shard_map/psum | solution.py:128
  57.8 21.4 %copy-start.38 = (f32[896]{0:T(1024)}, f32[896]{0:T(1024)S(1)}, u32[]{:S(2)}) copy-start(f32[896]{0:T(1024)S(1)} %convert_element_type.240) | copy-start | bytes 10756
  58.5 17.7 %copy-start.48 = (f32[32]{0:T(128)}, f32[32]{0:T(128)S(1)}, u32[]{:S(2)}) copy-start(f32[32]{0:T(128)S(1)} %multiply_power_fusion) | copy-start | bytes 388
  59.1 114.7 %copy-start.50 = (pred[512]{0:T(512)(128)(4,1)}, pred[512]{0:T(512)(128)(4,1)S(1)}, u32[]{:S(2)}) copy-start(pred[512]{0:T(512)(128)(4,1)S(1)} %iota_compare_fusion.1) | copy-start | bytes 1540
  59.2 17.0 %copy-start.42 = (f32[512]{0:T(512)}, f32[512]{0:T(512)S(1)}, u32[]{:S(2)}) copy-start(f32[512]{0:T(512)S(1)} %iota_convert_fusion) | copy-start | bytes 6148
  59.5 16.7 %copy-start.16 = (f32[512,32]{0,1:T(8,128)}, f32[512,32]{0,1:T(8,128)S(1)}, u32[]{:S(2)}) copy-start(f32[512,32]{0,1:T(8,128)S(1)} %get-tuple-element.58) | copy-start | bytes 196612
  74.5 4.7 copy-start.44
  75.4 2.3 copy-start.22
  75.4 2.3 copy-start.24
  77.7 2.9 copy-start.2
  77.7 2.9 copy-start.34
  79.3 3.6 copy-start.36
  80.6 3.1 copy-start.6
  82.9 2.7 copy-start.11
  85.6 7.4 copy-start.54
  87.2 86.6 %all-to-all-start.2 = ((bf16[64,8,896]{2,1,0:T(8,128)(2,1)}), bf16[64,8,896]{2,1,0:T(8,128)(2,1)}, u32[]{:S(2)}, u32[]{:S(2)}) async-start(bf16[64,8,896]{2,1,0:T(8,128)(2,1)} %gather_fusion.2), calls=%async_computation.2 | async-start | bytes 1835008 | tf_op jit(solution)/shard_map/all_to_all | solution.py:84
  92.7 143.9 %all-reduce.10.cloned.1.call-start = ((), (), s32[]{:S(2)}) async-start(), calls=%async_computation.5 | async-start | bytes 1835008 | tf_op jit(solution)/shard_map/psum | solution.py:137
  93.0 69.1 %copy-start.32 = (f32[896]{0:T(1024)}, f32[896]{0:T(1024)S(1)}, u32[]{:S(2)}) copy-start(f32[896]{0:T(1024)S(1)} %convert_element_type.253) | copy-start | bytes 10756
  160.6 143.2 %copy-start.3 = (f32[512,896]{1,0:T(8,128)}, f32[512,896]{1,0:T(8,128)S(1)}, u32[]{:S(2)}) copy-start(f32[512,896]{1,0:T(8,128)S(1)} %get-tuple-element.40) | copy-start | bytes 5505028
  161.9 7.5 slice-start.5
  162.1 7.2 copy-start.12
  162.1 7.2 slice-start.6
  191.7 112.1 %all-reduce.12.cloned.1.call-start = ((), (), s32[]{:S(2)}) async-start(), calls=%async_computation.6 | async-start | bytes 3670016 | tf_op jit(solution)/shard_map/psum | solution.py:158
  191.8 6.0 copy-start.63
  204.1 174.5 %all-reduce.14.cloned.1.call-start = ((), (), s32[]{:S(2)}) async-start(), calls=%async_computation.7 | async-start | bytes 1835008 | tf_op jit(solution)/shard_map/psum | solution.py:201
  205.3 8.3 copy-start.13
  205.3 8.3 copy-start.64
  213.6 6.1 copy-start.51
  213.6 6.1 copy-start.62
  303.8 5.6 copy-start.5
  303.8 5.6 copy-start.33
  303.8 5.6 copy-start.41
  303.8 5.6 copy-start.47
  303.8 5.6 copy-start.52
  303.8 8.8 slice-start
  309.4 2.5 copy-start.7
  309.4 3.2 slice-start.1
  315.3 2.4 copy-start.23
  315.3 2.4 copy-start.25
  319.7 2.3 copy-start.17
  326.1 703.6 %all-reduce.16.cloned.1.call-start = ((), (), s32[]{:S(2)}) async-start(), calls=%async_computation.8 | async-start | bytes 59637760 | tf_op jit(solution)/shard_map/psum | solution.py:230
  327.5 3.0 copy-start.9
  344.8 11.3 %copy-start.45 = (f32[512]{0:T(512)S(1)}, f32[512]{0:T(512)}, u32[]{:S(2)}) copy-start(f32[512]{0:T(512)} %copy-done.44) | copy-start | bytes 6148
  347.7 43.6 %all-to-all-start.1 = ((bf16[64,2,3584]{2,1,0:T(2,128)(2,1)}), bf16[64,2,3584]{2,1,0:T(2,128)(2,1)}, u32[]{:S(2)}, u32[]{:S(2)}) async-start(bf16[64,2,3584]{2,1,0:T(2,128)(2,1)} %reshape.425), calls=%async_computation.1 | async-start | bytes 1835008 | tf_op jit(solution)/shard_map/all_to_all | solution.py:249
  390.0 9.6 copy-start.59
  390.0 10.3 copy-start.60
  391.3 304.6 %all-to-all-start.3 = ((bf16[64,2,3584]{2,1,0:T(2,128)(2,1)}), bf16[64,2,3584]{2,1,0:T(2,128)(2,1)S(1)}, u32[]{:S(2)}, u32[]{:S(2)}) async-start(bf16[64,2,3584]{2,1,0:T(2,128)(2,1)} %reshape.427), calls=%async_computation.3 | async-start | bytes 1835008 | tf_op jit(solution)/shard_map/all_to_all | solution.py:252
  410.7 3.8 copy-start.46
  1029.7 2.8 copy-start.21
  1029.7 3.5 copy-start.20
  1029.7 4.2 copy-start.10
  1035.0 8.6 copy-start.4
  1035.0 13.0 %slice-start.2 = ((s8[8716288]{0:T(1024)(128)(4,1)}), s8[4194304]{0:T(1024)(128)(4,1)S(1)}, s32[]{:S(2)}) async-start(s8[8716288]{0:T(1024)(128)(4,1)} %bitcast.469), calls=%async_computation.11 | async-start | bytes 8388608
  1035.0 14.6 %slice-start.3 = ((s8[8716288]{0:T(1024)(128)(4,1)}), s8[4194304]{0:T(1024)(128)(4,1)S(1)}, s32[]{:S(2)}) async-start(s8[8716288]{0:T(1024)(128)(4,1)} %bitcast.469), calls=%async_computation.12 | async-start | bytes 8388608
  1043.7 6.1 slice-start.4
  1049.8 3.5 copy-start.1
  (17 other events, 24.8 us)
Sparse Core Ops, SparseCore 0:
  85.7 73.0 all-reduce.7
  191.8 44.6 all-reduce.9
  239.0 64.7 all-reduce.11
  326.2 52.3 all-reduce.13
  382.7 646.9 all-reduce.15
